TPU v7x, 128 devices: a whole 4x4x4 slice. The times are simulated.
128 devices in a mesh: wide: 32 (over z, y_lo, x), narrow: 4 (over y_hi, core).
Axes of the slice: x: 4, y: 4 (y_hi: 2, y_lo: 2; y = y_hi * 2 + y_lo), z: 4, core: 2. Of those that a mesh axis runs over, the one named last changes fastest.
Arguments:
- hidden: bfloat16 [512, 4, 8192], P('narrow', None, 'wide'), may hold values from -0.1796875 to 0.1796875
- grad_out: bfloat16 [512, 8192], P('narrow', 'wide'), may hold values from -6 to 6
- weight_base: bfloat16 [32768, 8192], P('narrow', 'wide'), may hold values from -0.0625 to 0.0625
- block_scale: bfloat16 [2048, 512], P('narrow', 'wide'), may hold values from 0.25 to 4
Outputs:
- grad_hidden: bfloat16 [512, 4, 8192], P('narrow', None, 'wide')
- grad_weight: bfloat16 [8192, 4, 8192], P('narrow', None, 'wide')
All inputs are finite; a program needn't handle non-finite values.
Results may differ from a plain program's by a relative error of at most 0.0049.
Values may be sent and summed in bfloat16 or wider, within the bound.
No kernel may reach another device: no remote copies, remote signals or barrier semaphores. Data moves between devices by JAX's collectives and lax.ppermute only.
A program may use at most 192 MiB of HBM per device.

v0:
```python
import jax
import jax.numpy as jnp
from jax import lax
from jax.sharding import PartitionSpec as P


def from_everyone(shard, axis):
    length = lax.axis_size(axis)
    return lax.all_to_all(
        jnp.broadcast_to(shard[None], (length, *shard.shape)), axis, 0, 0, tiled=True
    )


def joined_along(parts, dim):
    shape = list(parts.shape[1:])
    shape[dim] *= parts.shape[0]
    return jnp.moveaxis(parts, 0, dim).reshape(shape)


def gathered_copies(shard, axis, dim):
    parts = from_everyone(shard, axis)
    return joined_along(parts, dim)


def apply_scales(values, scales):
    height, breadth = values.shape
    widened = jnp.repeat(scales, 16, axis=1).astype(jnp.float32)
    blocked = values.reshape(height // 16, 16, breadth).astype(jnp.float32)
    blocked = blocked * widened[:, None, :]
    return blocked.reshape(height, breadth).astype(jnp.bfloat16)


def per_device(hidden, grad_out, weight_base, block_scale):
    tokens_here, groups, slice_width = hidden.shape
    row_values, row_scales = (
        lax.all_to_all(weight_base, "wide", split_axis=0, concat_axis=1, tiled=True),
        lax.all_to_all(block_scale, "wide", split_axis=0, concat_axis=1, tiled=True),
    )
    values_all, scales_all = (
        lax.all_gather(row_values, "narrow", axis=0, tiled=True),
        lax.all_gather(row_scales, "narrow", axis=0, tiled=True),
    )
    effective = apply_scales(values_all, scales_all)
    contract_last = (((1,), (1,)), ((), ()))
    incoming = gathered_copies(grad_out, "wide", 1)
    summed = lax.dot_general(incoming, effective, contract_last, preferred_element_type=jnp.float32)
    summed, gathered = (summed, incoming)
    grad_hidden = summed.astype(jnp.bfloat16).reshape(tokens_here, groups, slice_width)
    columns_mine = lax.all_to_all(gathered, "narrow", split_axis=1, concat_axis=0, tiled=True)
    hidden_all = lax.all_gather(
        hidden.reshape(tokens_here, groups * slice_width), "narrow", axis=0, tiled=True
    )
    product = lax.dot_general(
        columns_mine, hidden_all, (((0,), (0,)), ((), ())), preferred_element_type=jnp.float32
    )
    grad_weight = product.astype(jnp.bfloat16).reshape(product.shape[0], groups, slice_width)
    return (grad_hidden, grad_weight)


def solution(mesh):
    return jax.shard_map(
        per_device,
        mesh=mesh,
        in_specs=(
            P("narrow", None, "wide"),
            P("narrow", "wide"),
            P("narrow", "wide"),
            P("narrow", "wide"),
        ),
        out_specs=(P("narrow", None, "wide"), P("narrow", None, "wide")),
        check_vma=False,
    )
```

profile of v0, /device:TPU:1, one launch (start us, length us, event | category | flops | bytes accessed | tf_op | source)
XLA Modules:
  0.0 282.5 jit_solution(4466259191748090938)
XLA Ops:
  7.2 0.0 copy-start
  7.2 10.0 %all-to-all-start = ((bf16[32,256,256]{2,1,0:T(8,128)(2,1)}), bf16[32,256,256]{2,1,0:T(8,128)(2,1)}, u32[]{:S(2)}, u32[]{:S(2)}) async-start(bf16[32,256,256]{2,1,0:T(8,128)(2,1)} %bitcast.33), calls=%async_computation | async-start | bytes 8388608 | tf_op jit(solution)/shard_map/all_to_all | solution.py:36
  17.2 0.0 all-gather.5.cloned.1.call-start
  17.2 0.0 copy-done
  17.2 0.7 copy.34
  18.0 0.0 all-gather.5.cloned.1.call-update
  18.0 0.0 all-gather.3.cloned.1.call-start
  18.1 53.2 %all-to-all-done = bf16[32,256,256]{2,1,0:T(8,128)(2,1)} async-done(((bf16[32,256,256]{2,1,0:T(8,128)(2,1)}), bf16[32,256,256]{2,1,0:T(8,128)(2,1)}, u32[]{:S(2)}, u32[]{:S(2)}) %all-to-all-start) | async-done | bytes 4194336 | tf_op jit(solution)/shard_map/all_to_all | solution.py:36
  71.2 6.5 %copy.23 = bf16[256,32,256]{0,2,1:T(8,128)(2,1)} copy(bf16[256,32,256]{2,0,1:T(8,128)(2,1)} %bitcast.1) | data formatting | bytes 8388608 | tf_op jit(solution)/shard_map/all_to_all | solution.py:36
  77.7 0.0 copy-start.2
  77.7 0.0 copy-start.1
  77.7 0.0 all-gather.3.cloned.1.call-update
  77.8 0.7 copy-done.2
  78.5 0.1 all_to_all.49
  78.6 0.1 copy.36
  78.7 0.7 reshape.41
  79.4 10.3 %all-to-all-start.1 = ((bf16[32,2,128]{2,1,0:T(2,128)(2,1)}), bf16[32,2,128]{2,1,0:T(2,128)(2,1)S(1)}, u32[]{:S(2)}, u32[]{:S(2)}) async-start(bf16[32,2,128]{2,1,0:T(2,128)(2,1)} %reshape.41), calls=%async_computation.1 | async-start | bytes 32768 | tf_op jit(solution)/shard_map/all_to_all | solution.py:37
  89.8 0.0 copy-done.1
  89.8 0.1 copy.29
  89.9 6.9 %all-to-all-done.1 = bf16[32,2,128]{2,1,0:T(2,128)(2,1)S(1)} async-done(((bf16[32,2,128]{2,1,0:T(2,128)(2,1)}), bf16[32,2,128]{2,1,0:T(2,128)(2,1)S(1)}, u32[]{:S(2)}, u32[]{:S(2)}) %all-to-all-start.1) | async-done | bytes 16416 | tf_op jit(solution)/shard_map/all_to_all | solution.py:37
  96.8 0.5 broadcast_in_dim.5
  97.3 33.7 %all_to_all.62 = bf16[32,128,256]{1,2,0:T(8,128)(2,1)} all-to-all(bf16[32,128,256]{1,2,0:T(8,128)(2,1)S(1)} %broadcast_in_dim.5), channel_id=1, replica_groups=mesh['wide'=32,'narrow'=4] {'wide'}, dimensions={0} | all-to-all | bytes 4194304 | tf_op jit(solution)/shard_map/all_to_all | solution.py:9
  131.0 6.6 %all-to-all-start.3 = ((bf16[128,4,2048]{0,2,1:T(8,128)(2,1)}), bf16[128,4,2048]{0,2,1:T(8,128)(2,1)}, u32[]{:S(2)}, u32[]{:S(2)}) async-start(bf16[128,4,2048]{0,2,1:T(8,128)(2,1)} %bitcast.11), calls=%async_computation.3 | async-start | bytes 4194304 | tf_op jit(solution)/shard_map/all_to_all | solution.py:49
  137.7 0.1 reshape.42
  137.8 0.1 copy.33
  137.9 51.1 %all_gather.10 = bf16[64,512]{1,0:T(8,128)(2,1)S(1)} all-gather(bf16[16,512]{1,0:T(8,128)(2,1)S(1)} %copy.33), channel_id=1, replica_groups=mesh['wide'=32,'narrow'=4] {'narrow'}, dimensions={0}, use_global_device_ids=true | all-gather | bytes 81920 | tf_op jit(solution)/shard_map/all_gather | solution.py:41
  189.0 0.1 copy.26
  189.1 2.3 broadcast_in_dim.4
  191.4 3.2 %copy.27 = f32[64,8192]{1,0:T(8,128)S(1)} copy(f32[64,8192]{0,1:T(8,128)} %bitcast.32) | data formatting | bytes 4194304 | tf_op jit(solution)/shard_map/convert_element_type | solution.py:27
  194.6 11.2 %mul.11 = f32[64,16,8192]{2,1,0:T(8,128)} broadcast(f32[64,8192]{1,0:T(8,128)S(1)} %copy.27), dimensions={0,2} | broadcast | bytes 35651584 | tf_op jit(solution)/shard_map/mul | solution.py:29
  205.8 33.5 %copy.28 = f32[1024,8192]{0,1:T(8,128)} copy(f32[1024,8192]{1,0:T(8,128)} %bitcast.30) | data formatting | bytes 67108864 | tf_op jit(solution)/shard_map/mul | solution.py:29
  239.3 0.0 all-to-all-done.3
  239.3 2.9 %copy.30 = bf16[4,128,2048]{2,1,0:T(8,128)(2,1)S(1)} copy(bf16[4,128,2048]{1,2,0:T(8,128)(2,1)} %bitcast.12) | data formatting | bytes 4194304 | tf_op jit(solution)/shard_map/all_to_all | solution.py:49
  242.3 0.0 all-gather.5.cloned.1.call-done
  242.3 5.7 %convolution_convert_fusion = bf16[2048,1024]{0,1:T(8,128)(2,1)} fusion(bf16[512,2048]{1,0:T(8,128)(2,1)S(1)} %bitcast.35, bf16[512,1024]{1,0:T(8,128)(2,1)} %all-gather.5.cloned.1.call-done), kind=kOutput, calls=%fused_computation.2 | convolution fusion | flops 2149580800 | bytes 7340032 | tf_op jit(solution)/shard_map/dot_general | solution.py:53
  248.0 7.4 %copy.32 = bf16[2048,4,256]{2,1,0:T(4,128)(2,1)} copy(bf16[2048,4,256]{0,2,1:T(8,128)(2,1)} %bitcast.34) | data formatting | bytes 8388608
  255.4 0.0 all-gather.3.cloned.1.call-done
  255.4 19.3 %fusion.1 = bf16[1024,128]{1,0:T(8,128)(2,1)S(1)} fusion(bf16[128,8192]{0,1:T(8,128)(2,1)} %bitcast.8, f32[1024,8192]{0,1:T(8,128)} %copy.28, bf16[1024,8192]{0,1:T(8,128)(2,1)} %all-gather.3.cloned.1.call-done), kind=kOutput, calls=%fused_computation.3 | convolution fusion | flops 2172780544 | bytes 52690944 | tf_op jit(solution)/shard_map/dot_general | solution.py:46
  274.7 0.9 copy.31
Async XLA Ops:
  7.2 10.1 %copy-start = (bf16[128,4,256]{2,1,0:T(4,128)(2,1)S(1)}, bf16[128,4,256]{2,1,0:T(4,128)(2,1)}, u32[]{:S(2)}) copy-start(bf16[128,4,256]{2,1,0:T(4,128)(2,1)} %param.4) | copy-start | bytes 786436
  7.2 64.1 %all-to-all-start = ((bf16[32,256,256]{2,1,0:T(8,128)(2,1)}), bf16[32,256,256]{2,1,0:T(8,128)(2,1)}, u32[]{:S(2)}, u32[]{:S(2)}) async-start(bf16[32,256,256]{2,1,0:T(8,128)(2,1)} %bitcast.33), calls=%async_computation | async-start | bytes 8388608 | tf_op jit(solution)/shard_map/all_to_all | solution.py:36
  17.2 225.1 %all-gather.5.cloned.1.call-start = ((), (), s32[]{:S(2)}) async-start(), calls=%async_computation.5 | async-start | bytes 1310720 | tf_op jit(solution)/shard_map/all_gather | solution.py:50
  18.0 237.4 %all-gather.3.cloned.1.call-start = ((), (), s32[]{:S(2)}) async-start(), calls=%async_computation.4 | async-start | bytes 20971520 | tf_op jit(solution)/shard_map/all_gather | solution.py:40
  77.7 0.7 copy-start.2
  77.7 12.0 %copy-start.1 = (bf16[128,256]{1,0:T(8,128)(2,1)S(1)}, bf16[128,256]{1,0:T(8,128)(2,1)}, u32[]{:S(2)}) copy-start(bf16[128,256]{1,0:T(8,128)(2,1)} %param.5) | copy-start | bytes 196612
  79.4 17.4 %all-to-all-start.1 = ((bf16[32,2,128]{2,1,0:T(2,128)(2,1)}), bf16[32,2,128]{2,1,0:T(2,128)(2,1)S(1)}, u32[]{:S(2)}, u32[]{:S(2)}) async-start(bf16[32,2,128]{2,1,0:T(2,128)(2,1)} %reshape.41), calls=%async_computation.1 | async-start | bytes 32768 | tf_op jit(solution)/shard_map/all_to_all | solution.py:37
  131.0 108.3 %all-to-all-start.3 = ((bf16[128,4,2048]{0,2,1:T(8,128)(2,1)}), bf16[128,4,2048]{0,2,1:T(8,128)(2,1)}, u32[]{:S(2)}, u32[]{:S(2)}) async-start(bf16[128,4,2048]{0,2,1:T(8,128)(2,1)} %bitcast.11), calls=%async_computation.3 | async-start | bytes 4194304 | tf_op jit(solution)/shard_map/all_to_all | solution.py:49
Sparse Core Ops, SparseCore 0:
  20.3 52.2 all-gather.4
  77.9 162.2 all-gather.2
where the time goes:
time: 284 us; the launch traced here: 282 us
  blocking collectives  84.9 us (30%)
  local copies, waits for them, and re-layouts  71.2 us (25%)
  waiting for transfers between devices  60.2 us (21%)
  starting transfers between devices  27.1 us (10%)
  matrix products  25 us (9%)
  between operations  14.2 us (5%)
    all_to_all x1, waiting for transfers between devices, per_device(): lax.all_to_all(weight_base, 'wide', split_axis=0, concat_axis=1, tiled=True)  53.2 us
    all_gather x1, blocking collectives, per_device(): lax.all_gather(row_scales, 'narrow', axis=0, tiled=True)  51.1 us
    mul x2, local copies, waits for them, and re-layouts, apply_scales(): blocked = blocked * widened[:, None, :]  44.7 us
    all_to_all x1, blocking collectives, from_everyone(): lax.all_to_all(jnp.broadcast_to(shard[None], (length, *shard.shape)), axi...  33.7 us
    dot_general x1, matrix products, per_device(): lax.dot_general(incoming, effective, contract_last, preferred_element_typ...  19.3 us
    unnamed x12, local copies, waits for them, and re-layouts  10.7 us
    all_to_all x1, starting transfers between devices, per_device(): lax.all_to_all(block_scale, 'wide', split_axis=0, concat_axis=1, tiled=True)  10.3 us
    all_to_all x1, starting transfers between devices, per_device(): lax.all_to_all(weight_base, 'wide', split_axis=0, concat_axis=1, tiled=True)  10 us
  transfers between devices with their start and end apart: 5, of which 2 were waited for; matrix products, arithmetic and copies ran while one was open for 27% of the time, Pallas kernels for 0%

commit v1 on v0

--- a/solution.py
+++ b/solution.py
@@ -2,6 +2,15 @@
 import jax.numpy as jnp
 from jax import lax
 from jax.sharding import PartitionSpec as P
+
+
+def map_positions(inner_x, link_axis, on_dim):
+    grid = []
+    for _ in range(lax.axis_size(link_axis)):
+        grid.append(inner_x)
+    return jnp.concatenate(
+        lax.all_to_all(jnp.stack(grid, 0), axis_name=link_axis, concat_axis=0, split_axis=0), on_dim
+    )
 
 
 def from_everyone(shard, axis):
@@ -38,7 +47,7 @@
     )
     values_all, scales_all = (
         lax.all_gather(row_values, "narrow", axis=0, tiled=True),
-        lax.all_gather(row_scales, "narrow", axis=0, tiled=True),
+        map_positions(row_scales, "narrow", 0),
     )
     effective = apply_scales(values_all, scales_all)
     contract_last = (((1,), (1,)), ((), ()))

time: 284 us -> 269 us (0.947)
  blocking collectives: 84.9 us -> 51.2 us
  waiting for transfers between devices: 60.2 us -> 84.4 us
  starting transfers between devices: 27.1 us -> 22 us
    all_gather x1 -> x0, blocking collectives: 51.1 us -> none  [per_device(): lax.all_gather(row_scales, 'narrow', axis=0, tiled=True)]
    all_gather x1, waiting for transfers between devices: 0.01 us -> 25.6 us  [per_device(): lax.all_gather(row_values, 'narrow', axis=0, tiled=True)]
    all_to_all x0 -> x1, blocking collectives: none -> 17.3 us  [per_device(): lax.all_to_all(block_scale, 'wide', split_axis=0, concat_axis=1, tiled=True)]
    all_to_all x1, starting transfers between devices: 10.3 us -> 6.08 us  [map_positions(): lax.all_to_all(jnp.stack(grid, 0), axis_name=link_axis, concat_axis=0, sp...]
  transfers between devices with their start and end apart: 5 -> 5, of which waited for: 2 -> 3; matrix products, arithmetic and copies ran while one was open for 27% -> 28% of each run, Pallas kernels for 0% -> 0%
where the time goes in v1:
time: 269 us; the launch traced here: 268 us
  waiting for transfers between devices  84.4 us (31%)
  local copies, waits for them, and re-layouts  70.9 us (26%)
  blocking collectives  51.2 us (19%)
  matrix products  25 us (9%)
  starting transfers between devices  22 us (8%)
  between operations  14.1 us (5%)
    all_to_all x1, waiting for transfers between devices, per_device(): lax.all_to_all(weight_base, 'wide', split_axis=0, concat_axis=1, tiled=True)  53.2 us
    mul x2, local copies, waits for them, and re-layouts, apply_scales(): blocked = blocked * widened[:, None, :]  44.7 us
    all_to_all x1, blocking collectives, from_everyone(): lax.all_to_all(jnp.broadcast_to(shard[None], (length, *shard.shape)), axi...  33.9 us
    all_gather x1, waiting for transfers between devices, per_device(): lax.all_gather(row_values, 'narrow', axis=0, tiled=True)  25.6 us
    dot_general x1, matrix products, per_device(): lax.dot_general(incoming, effective, contract_last, preferred_element_typ...  19.3 us
    all_to_all x1, blocking collectives, per_device(): lax.all_to_all(block_scale, 'wide', split_axis=0, concat_axis=1, tiled=True)  17.3 us
    unnamed x12, local copies, waits for them, and re-layouts  10.1 us
    all_to_all x1, starting transfers between devices, per_device(): lax.all_to_all(weight_base, 'wide', split_axis=0, concat_axis=1, tiled=True)  10 us
  transfers between devices with their start and end apart: 5, of which 3 were waited for; matrix products, arithmetic and copies ran while one was open for 28% of the time, Pallas kernels for 0%

profile of v1, /device:TPU:1, one launch (start us, length us, event | category | flops | bytes accessed | tf_op | source)
XLA Modules:
  0.0 267.6 jit_solution(6495088383972399284)
XLA Ops:
  7.2 0.0 copy-start
  7.2 10.0 %all-to-all-start = ((bf16[32,256,256]{2,1,0:T(8,128)(2,1)}), bf16[32,256,256]{2,1,0:T(8,128)(2,1)}, u32[]{:S(2)}, u32[]{:S(2)}) async-start(bf16[32,256,256]{2,1,0:T(8,128)(2,1)} %bitcast.36), calls=%async_computation | async-start | bytes 8388608 | tf_op jit(solution)/shard_map/all_to_all | solution.py:45
  17.2 0.0 all-gather.5.cloned.1.call-start
  17.2 0.0 copy-done
  17.2 0.7 copy.34
  18.0 0.0 all-gather.5.cloned.1.call-update
  18.0 0.0 all-gather.3.cloned.1.call-start
  18.1 53.2 %all-to-all-done = bf16[32,256,256]{2,1,0:T(8,128)(2,1)} async-done(((bf16[32,256,256]{2,1,0:T(8,128)(2,1)}), bf16[32,256,256]{2,1,0:T(8,128)(2,1)}, u32[]{:S(2)}, u32[]{:S(2)}) %all-to-all-start) | async-done | bytes 4194336 | tf_op jit(solution)/shard_map/all_to_all | solution.py:45
  71.2 6.5 %copy.23 = bf16[256,32,256]{0,2,1:T(8,128)(2,1)} copy(bf16[256,32,256]{2,0,1:T(8,128)(2,1)} %bitcast.1) | data formatting | bytes 8388608 | tf_op jit(solution)/shard_map/all_to_all | solution.py:45
  77.7 0.0 copy-start.2
  77.7 0.0 copy-start.1
  77.7 0.0 all-gather.3.cloned.1.call-update
  77.8 0.7 copy-done.2
  78.5 0.1 all_to_all.50
  78.6 0.1 copy.36
  78.7 0.1 reshape.48
  78.8 17.3 %all_to_all.64 = bf16[32,2,128]{2,1,0:T(2,128)(2,1)S(1)} all-to-all(bf16[32,2,128]{2,1,0:T(2,128)(2,1)S(1)} %reshape.48), channel_id=1, replica_groups=mesh['wide'=32,'narrow'=4] {'wide'}, dimensions={0} | all-to-all | bytes 32768 | tf_op jit(solution)/shard_map/all_to_all | solution.py:46
  96.1 0.1 reshape.49
  96.2 0.1 copy.33
  96.3 0.7 stack.10
  97.0 6.1 %all-to-all-start.2 = ((bf16[4,16,512]{2,1,0:T(8,128)(2,1)}), bf16[4,16,512]{2,1,0:T(8,128)(2,1)S(1)}, u32[]{:S(2)}, u32[]{:S(2)}) async-start(bf16[4,16,512]{2,1,0:T(8,128)(2,1)} %stack.10), calls=%async_computation.2 | async-start | bytes 131072 | tf_op jit(solution)/shard_map/all_to_all | solution.py:12
  103.0 0.0 copy-done.1
  103.0 0.1 copy.29
  103.1 5.5 %all-to-all-done.2 = bf16[4,16,512]{2,1,0:T(8,128)(2,1)S(1)} async-done(((bf16[4,16,512]{2,1,0:T(8,128)(2,1)}), bf16[4,16,512]{2,1,0:T(8,128)(2,1)S(1)}, u32[]{:S(2)}, u32[]{:S(2)}) %all-to-all-start.2) | async-done | bytes 65568 | tf_op jit(solution)/shard_map/all_to_all | solution.py:12
  108.7 0.5 broadcast_in_dim.5
  109.1 33.9 %all_to_all.65 = bf16[32,128,256]{1,2,0:T(8,128)(2,1)} all-to-all(bf16[32,128,256]{1,2,0:T(8,128)(2,1)S(1)} %broadcast_in_dim.5), channel_id=1, replica_groups=mesh['wide'=32,'narrow'=4] {'wide'}, dimensions={0} | all-to-all | bytes 4194304 | tf_op jit(solution)/shard_map/all_to_all | solution.py:18
  143.0 5.8 %all-to-all-start.4 = ((bf16[128,4,2048]{0,2,1:T(8,128)(2,1)}), bf16[128,4,2048]{0,2,1:T(8,128)(2,1)}, u32[]{:S(2)}, u32[]{:S(2)}) async-start(bf16[128,4,2048]{0,2,1:T(8,128)(2,1)} %bitcast.12), calls=%async_computation.4 | async-start | bytes 4194304 | tf_op jit(solution)/shard_map/all_to_all | solution.py:58
  148.9 0.1 copy.26
  149.0 2.3 broadcast_in_dim.4
  151.3 2.8 %copy.27 = f32[64,8192]{1,0:T(8,128)S(1)} copy(f32[64,8192]{0,1:T(8,128)} %bitcast.35) | data formatting | bytes 4194304 | tf_op jit(solution)/shard_map/convert_element_type | solution.py:36
  154.1 11.2 %mul.11 = f32[64,16,8192]{2,1,0:T(8,128)} broadcast(f32[64,8192]{1,0:T(8,128)S(1)} %copy.27), dimensions={0,2} | broadcast | bytes 35651584 | tf_op jit(solution)/shard_map/mul | solution.py:38
  165.3 33.5 %copy.28 = f32[1024,8192]{0,1:T(8,128)} copy(f32[1024,8192]{1,0:T(8,128)} %bitcast.33) | data formatting | bytes 67108864 | tf_op jit(solution)/shard_map/mul | solution.py:38
  198.8 0.0 all-to-all-done.4
  198.8 2.9 %copy.30 = bf16[4,128,2048]{2,1,0:T(8,128)(2,1)S(1)} copy(bf16[4,128,2048]{1,2,0:T(8,128)(2,1)} %bitcast.13) | data formatting | bytes 4194304 | tf_op jit(solution)/shard_map/all_to_all | solution.py:58
  201.8 0.0 all-gather.5.cloned.1.call-done
  201.8 5.7 %convolution_convert_fusion = bf16[2048,1024]{0,1:T(8,128)(2,1)} fusion(bf16[512,2048]{1,0:T(8,128)(2,1)S(1)} %bitcast.38, bf16[512,1024]{1,0:T(8,128)(2,1)} %all-gather.5.cloned.1.call-done), kind=kOutput, calls=%fused_computation.2 | convolution fusion | flops 2149580800 | bytes 7340032 | tf_op jit(solution)/shard_map/dot_general | solution.py:62
  207.5 7.4 %copy.32 = bf16[2048,4,256]{2,1,0:T(4,128)(2,1)} copy(bf16[2048,4,256]{0,2,1:T(8,128)(2,1)} %bitcast.37) | data formatting | bytes 8388608
  214.9 25.6 %all-gather.3.cloned.1.call-done = bf16[1024,8192]{0,1:T(8,128)(2,1)} async-done(((bf16[256,8192]{0,1:T(8,128)(2,1)}), bf16[1024,8192]{0,1:T(8,128)(2,1)}) %all-gather.3.cloned.1.call-update) | async-done | bytes 16777232 | tf_op jit(solution)/shard_map/all_gather | solution.py:49
  240.6 19.3 %fusion.1 = bf16[1024,128]{1,0:T(8,128)(2,1)S(1)} fusion(bf16[128,8192]{0,1:T(8,128)(2,1)} %bitcast.9, f32[1024,8192]{0,1:T(8,128)} %copy.28, bf16[1024,8192]{0,1:T(8,128)(2,1)} %all-gather.3.cloned.1.call-done), kind=kOutput, calls=%fused_computation.3 | convolution fusion | flops 2172780544 | bytes 52690944 | tf_op jit(solution)/shard_map/dot_general | solution.py:55
  259.9 0.9 copy.31
  (1 shorter events, 0.0 us)
Async XLA Ops:
  7.2 10.1 %copy-start = (bf16[128,4,256]{2,1,0:T(4,128)(2,1)S(1)}, bf16[128,4,256]{2,1,0:T(4,128)(2,1)}, u32[]{:S(2)}) copy-start(bf16[128,4,256]{2,1,0:T(4,128)(2,1)} %param.4) | copy-start | bytes 786436
  7.2 64.1 %all-to-all-start = ((bf16[32,256,256]{2,1,0:T(8,128)(2,1)}), bf16[32,256,256]{2,1,0:T(8,128)(2,1)}, u32[]{:S(2)}, u32[]{:S(2)}) async-start(bf16[32,256,256]{2,1,0:T(8,128)(2,1)} %bitcast.36), calls=%async_computation | async-start | bytes 8388608 | tf_op jit(solution)/shard_map/all_to_all | solution.py:45
  17.2 184.6 %all-gather.5.cloned.1.call-start = ((), (), s32[]{:S(2)}) async-start(), calls=%async_computation.6 | async-start | bytes 1310720 | tf_op jit(solution)/shard_map/all_gather | solution.py:59
  18.0 222.6 %all-gather.3.cloned.1.call-start = ((), (), s32[]{:S(2)}) async-start(), calls=%async_computation.5 | async-start | bytes 20971520 | tf_op jit(solution)/shard_map/all_gather | solution.py:49
  77.7 0.7 copy-start.2
  77.7 25.3 %copy-start.1 = (bf16[128,256]{1,0:T(8,128)(2,1)S(1)}, bf16[128,256]{1,0:T(8,128)(2,1)}, u32[]{:S(2)}) copy-start(bf16[128,256]{1,0:T(8,128)(2,1)} %param.5) | copy-start | bytes 196612
  97.0 11.7 %all-to-all-start.2 = ((bf16[4,16,512]{2,1,0:T(8,128)(2,1)}), bf16[4,16,512]{2,1,0:T(8,128)(2,1)S(1)}, u32[]{:S(2)}, u32[]{:S(2)}) async-start(bf16[4,16,512]{2,1,0:T(8,128)(2,1)} %stack.10), calls=%async_computation.2 | async-start | bytes 131072 | tf_op jit(solution)/shard_map/all_to_all | solution.py:12
  143.0 55.8 %all-to-all-start.4 = ((bf16[128,4,2048]{0,2,1:T(8,128)(2,1)}), bf16[128,4,2048]{0,2,1:T(8,128)(2,1)}, u32[]{:S(2)}, u32[]{:S(2)}) async-start(bf16[128,4,2048]{0,2,1:T(8,128)(2,1)} %bitcast.12), calls=%async_computation.4 | async-start | bytes 4194304 | tf_op jit(solution)/shard_map/all_to_all | solution.py:58
Sparse Core Ops, SparseCore 0:
  20.3 52.2 all-gather.4
  77.9 162.6 all-gather.2
